TPU v7x, 32 devices: a whole 2x2x4 slice. The times are simulated.
32 devices in a mesh: dp: 2 (over core), dom: 16 (over z, y, x).
Axes of the slice: x: 2, y: 2, z: 4, core: 2. Of those that a mesh axis runs over, the one named last changes fastest.
Arguments:
- features: bfloat16 [2, 6144, 512], P('dp', 'dom'), may hold values from -12 to 12
- tile_mask: int32 [2, 48, 18], P('dp', 'dom'), may hold values from 0 to 1, as said below
- cotangent: bfloat16 [2, 6144, 512], P('dp', 'dom'), may hold values from -6 to 6
- w_query: bfloat16 [512, 512], replicated, may hold values from -1 to 1
- w_key: bfloat16 [512, 512], replicated, may hold values from -1 to 1
- w_value: bfloat16 [512, 512], replicated, may hold values from -0.25 to 0.25
- w_out: bfloat16 [512, 512], replicated, may hold values from -0.25 to 0.25
Outputs:
- attended: bfloat16 [2, 6144, 512], P('dp', 'dom')
- grad_features: bfloat16 [2, 6144, 512], P('dp', 'dom')
- grad_query: float32 [512, 512], replicated
- grad_key: float32 [512, 512], replicated
- grad_value: float32 [512, 512], replicated
- grad_out: float32 [512, 512], replicated
Inputs may be any that keep to these rules, and one draw needn't show every extreme that they name: `tile_mask`: 0 or 1; the share of ones differs between tile groups, from about a quarter to all.
All inputs are finite; a program needn't handle non-finite values.
Results may differ from a plain program's by a relative error of at most 0.023.
Values may be sent and summed in bfloat16 or wider, within the bound.
No kernel may reach another device: no remote copies, remote signals or barrier semaphores. Data moves between devices by JAX's collectives and lax.ppermute only.
A program may use at most 128 MiB of HBM per device.

v0:
```python
import jax
import jax.numpy as jnp
from jax import lax
from jax.sharding import PartitionSpec as P

HEADS = 8
HEAD_DIM = 64
TILE = 128
TILE_DEV = 3
NB = 3
CANDT = 18


def with_halo(block, sides, width):
    for axis, dim in sides:
        count = lax.axis_size(axis)
        forward = [(i, i + 1) for i in range(count - 1)]
        forward.append((count - 1, 0))
        backward = [(target, source) for source, target in forward]
        low = lax.ppermute(
            lax.slice_in_dim(block, block.shape[dim] - width, None, axis=dim), axis, forward
        )
        high = lax.ppermute(lax.slice_in_dim(block, 0, width, axis=dim), axis, backward)
        block = jnp.concatenate([low, block, high], axis=dim)
    return block


def from_partner(value, axis, distance):
    mask = 2**distance
    pairs = [(source, source ^ mask) for source in range(lax.axis_size(axis))]
    return lax.ppermute(value, axis, pairs)


def candidate_blocks(block):
    block_rows = block.shape[0]
    near = with_halo(block, (("dom", 0),), block_rows)
    pieces = [block, near[:block_rows], near[2 * block_rows :]]
    levels = lax.axis_size("dom").bit_length() - 1
    for bit_step in range(NB):
        pieces.append(from_partner(block, "dom", levels - 1 - bit_step))
    return pieces


def returned_sum(grad_parts):
    block_rows = grad_parts.shape[1]
    outgoing = jnp.concatenate([grad_parts[1], grad_parts[2]], 0)
    returned = with_halo(outgoing, (("dom", 0),), block_rows)
    summed = grad_parts[0] + returned[:block_rows] + returned[3 * block_rows :]
    levels = lax.axis_size("dom").bit_length() - 1
    for bit_step in range(NB):
        summed = summed + from_partner(grad_parts[3 + bit_step], "dom", levels - 1 - bit_step)
    return summed


def joined(stacked_parts, width_all):
    return jnp.transpose(stacked_parts, (1, 0, 2)).reshape(stacked_parts.shape[1], width_all)


def per_device(features, tile_mask, cotangent, w_query, w_key, w_value, w_out):
    node_rows = features[0]
    block_rows = node_rows.shape[0]
    width_all = node_rows.shape[1]
    highest = lax.Precision.HIGHEST
    factor = HEAD_DIM ** (-0.5)
    w_both = jnp.concatenate([w_key, w_value], 1)
    q_rows = jnp.dot(node_rows, w_query, preferred_element_type=jnp.float32).astype(jnp.bfloat16)
    kv_rows = jnp.dot(node_rows, w_both, preferred_element_type=jnp.float32).astype(jnp.bfloat16)
    pieces = candidate_blocks(node_rows)
    remote = jnp.dot(
        jnp.concatenate(pieces[1:], 0), w_both, preferred_element_type=jnp.float32
    ).astype(jnp.bfloat16)
    cand_kv = jnp.concatenate([kv_rows, remote], 0)
    key_count = cand_kv.shape[0]
    keys_all = cand_kv[:, :width_all]
    values_all = cand_kv[:, width_all:]
    own_tile = jnp.arange(CANDT)[None, :] == jnp.arange(TILE_DEV)[:, None]
    live_tiles = (tile_mask[0] == 1) | own_tile
    masking = jnp.where(live_tiles, 0.0, -1e30).astype(jnp.float32)
    cot_rows = cotangent[0]
    grad_o = jnp.dot(cot_rows, w_out.T, preferred_element_type=jnp.float32).astype(jnp.bfloat16)
    pair_cols = 2 * HEAD_DIM

    def head_pair(pair_index):
        col_start = pair_index * pair_cols
        q_pair = lax.dynamic_slice_in_dim(q_rows, col_start, pair_cols, 1).reshape(
            block_rows, 2, HEAD_DIM
        )
        k_pair = lax.dynamic_slice_in_dim(keys_all, col_start, pair_cols, 1).reshape(
            key_count, 2, HEAD_DIM
        )
        v_pair = lax.dynamic_slice_in_dim(values_all, col_start, pair_cols, 1).reshape(
            key_count, 2, HEAD_DIM
        )
        g_pair = lax.dynamic_slice_in_dim(grad_o, col_start, pair_cols, 1).reshape(
            block_rows, 2, HEAD_DIM
        )
        scores = (
            jnp.einsum("rhd,chd->hrc", q_pair, k_pair, preferred_element_type=jnp.float32) * factor
        )
        scores = scores.reshape(2, TILE_DEV, TILE, CANDT, TILE) + masking[None, :, None, :, None]
        scores = scores.reshape(2, block_rows, key_count)
        row_max = jnp.max(scores, axis=2, keepdims=True)
        exp_vals = jnp.exp(scores - row_max)
        prob_f32 = exp_vals / jnp.sum(exp_vals, axis=2, keepdims=True)
        prob_bf = prob_f32.astype(jnp.bfloat16)
        out_pair = jnp.einsum(
            "hrc,chd->rhd", prob_bf, v_pair, preferred_element_type=jnp.float32
        ).astype(jnp.bfloat16)
        grad_prob = jnp.einsum("rhd,chd->hrc", g_pair, v_pair, preferred_element_type=jnp.float32)
        row_delta = jnp.einsum(
            "rhd,rhd->hr", g_pair.astype(jnp.float32), out_pair.astype(jnp.float32)
        )
        grad_score = (prob_f32 * (grad_prob - row_delta[:, :, None]) * factor).astype(jnp.bfloat16)
        gq_pair = jnp.einsum(
            "hrc,chd->rhd", grad_score, k_pair, preferred_element_type=jnp.float32
        ).reshape(block_rows, pair_cols)
        gk_pair = jnp.einsum(
            "hrc,rhd->chd", grad_score, q_pair, preferred_element_type=jnp.float32
        ).reshape(key_count, pair_cols)
        gv_pair = jnp.einsum(
            "hrc,rhd->chd", prob_bf, g_pair, preferred_element_type=jnp.float32
        ).reshape(key_count, pair_cols)
        return (out_pair.reshape(block_rows, pair_cols), gq_pair, gk_pair, gv_pair)

    stacked = lax.map(head_pair, jnp.arange(HEADS // 2, dtype=jnp.int32))
    out_rows = joined(stacked[0], width_all)
    grad_q = joined(stacked[1], width_all)
    grad_k = joined(stacked[2], width_all)
    grad_v = joined(stacked[3], width_all)
    attended = jnp.dot(out_rows, w_out, preferred_element_type=jnp.float32).astype(jnp.bfloat16)
    grad_parts = jnp.concatenate([grad_k, grad_v], 1).reshape(3 + NB, block_rows, 2 * width_all)
    w_both32 = w_both.astype(jnp.float32)
    rows_f32 = node_rows.astype(jnp.float32)
    contrib = jnp.einsum("scf,df->scd", grad_parts, w_both32, precision=highest)
    kv_dx = returned_sum(contrib)
    cand_rows = (
        jnp.concatenate(pieces, 0).reshape(3 + NB, block_rows, width_all).astype(jnp.float32)
    )
    g_both = jnp.einsum("scd,scf->df", cand_rows, grad_parts, precision=highest)
    grad_x = jnp.dot(grad_q, w_query.astype(jnp.float32).T, precision=highest) + kv_dx
    g_query = jnp.dot(rows_f32.T, grad_q, precision=highest)
    g_out = jnp.dot(out_rows.T, cot_rows, preferred_element_type=jnp.float32)
    g_query, g_key, g_value, g_out = lax.psum(
        (g_query, g_both[:, :width_all], g_both[:, width_all:], g_out), ("dp", "dom")
    )
    return (attended[None], grad_x.astype(jnp.bfloat16)[None], g_query, g_key, g_value, g_out)


def solution(mesh):
    in_specs = (
        P("dp", "dom", None),
        P("dp", "dom", None),
        P("dp", "dom", None),
        P(),
        P(),
        P(),
        P(),
    )
    out_specs = (P("dp", "dom", None), P("dp", "dom", None), P(), P(), P(), P())
    return jax.shard_map(
        per_device, mesh=mesh, in_specs=in_specs, out_specs=out_specs, check_vma=False
    )
```

profile of v0, /device:TPU:0, one launch (start us, length us, event | category | flops | bytes accessed | tf_op | source)
XLA Modules:
  0.0 415.0 jit_solution(7876235823481581899)
XLA Ops:
  7.2 3.1 collective-permute-start.3
  10.4 2.6 collective-permute-start.2
  13.0 2.1 collective-permute-start.1
  15.1 1.4 collective-permute-start.4
  16.5 1.8 constant_dynamic-update-slice_fusion.18
  18.3 1.5 convolution_convert_fusion.5
  23.2 17.6 %collective-permute-done = bf16[384,512]{1,0:T(8,128)(2,1)} collective-permute-done((bf16[384,512]{1,0:T(8,128)(2,1)}, bf16[384,512]{1,0:T(8,128)(2,1)}, u32[]{:S(2)}, u32[]{:S(2)}) %collective-permute-start) | collective-permute-done | bytes 393248 | tf_op jit(solution)/shard_map/ppermute | solution.py:20
  40.8 1.8 constant_dynamic-update-slice_fusion.17
  42.7 1.8 constant_dynamic-update-slice_fusion.16
  44.5 1.8 constant_dynamic-update-slice_fusion.15
  46.3 1.8 constant_dynamic-update-slice_fusion.14
  48.1 1.8 constant_dynamic-update-slice_fusion.13
  49.9 2.2 convolution_convert_fusion.1
  52.1 3.8 pad_maximum_fusion
  55.9 110.8 %while.16 = (s32[]{:T(128)}, bf16[4,384,128]{1,2,0:T(8,128)(2,1)}, f32[4,384,128]{1,2,0:T(8,128)}, f32[4,2304,128]{1,2,0:T(8,128)}, f32[4,2304,128]{1,2,0:T(8,12...) while((s32[]{:T(128)}, bf16[4,384,128]{1,2,0:T(8,128)(2,1)}, ...), condition=%wide.region_3.4_spmd, body=%wide.region_0.3_spmd.sunk | while | flops 1378665984 | bytes 104414744 | solution.py:125
  60.7 2.5 copy.52
  63.2 7.1 %fusion.91 = (f32[2,384]{1,0:T(2,128)S(1)}, f32[2,384,2304]{2,1,0:T(8,128)}) fusion(f32[384,2304]{1,0:T(8,128)} %bitcast.170, bf16[384,2,64]{0,2,1:T(8,128)(2,1)S(1)} %bitcast.177, bf16[2304,2,64]{0,2,1:T(8,128)(2,1)S(1)} %bitcast.171), kind=kOutput, calls=%fused_computation.77.clone.1 | convolution fusion | flops 233572608 | bytes 11308032 | tf_op jit(solution)/shard_map/while/body/eval_jaxpr/sub | solution.py:103
  70.3 3.8 fusion.92
  74.1 1.2 fusion.93
  77.1 1.6 multiply_convert_fusion.2
  78.7 1.2 fusion.94
  82.0 1.7 constant_dynamic-update-slice_fusion.24
  88.4 2.5 copy.52
  90.9 7.1 %fusion.91 = (f32[2,384]{1,0:T(2,128)S(1)}, f32[2,384,2304]{2,1,0:T(8,128)}) fusion(f32[384,2304]{1,0:T(8,128)} %bitcast.170, bf16[384,2,64]{0,2,1:T(8,128)(2,1)S(1)} %bitcast.177, bf16[2304,2,64]{0,2,1:T(8,128)(2,1)S(1)} %bitcast.171), kind=kOutput, calls=%fused_computation.77.clone.1 | convolution fusion | flops 233572608 | bytes 11308032 | tf_op jit(solution)/shard_map/while/body/eval_jaxpr/sub | solution.py:103
  98.0 3.8 fusion.92
  101.9 1.2 fusion.93
  104.9 1.6 multiply_convert_fusion.2
  106.5 1.2 fusion.94
  109.8 1.6 constant_dynamic-update-slice_fusion.24
  116.2 2.5 copy.52
  118.7 7.1 %fusion.91 = (f32[2,384]{1,0:T(2,128)S(1)}, f32[2,384,2304]{2,1,0:T(8,128)}) fusion(f32[384,2304]{1,0:T(8,128)} %bitcast.170, bf16[384,2,64]{0,2,1:T(8,128)(2,1)S(1)} %bitcast.177, bf16[2304,2,64]{0,2,1:T(8,128)(2,1)S(1)} %bitcast.171), kind=kOutput, calls=%fused_computation.77.clone.1 | convolution fusion | flops 233572608 | bytes 11308032 | tf_op jit(solution)/shard_map/while/body/eval_jaxpr/sub | solution.py:103
  125.8 3.8 fusion.92
  129.6 1.2 fusion.93
  132.6 1.6 multiply_convert_fusion.2
  134.2 1.2 fusion.94
  137.5 1.6 constant_dynamic-update-slice_fusion.24
  143.8 2.5 copy.52
  146.3 7.1 %fusion.91 = (f32[2,384]{1,0:T(2,128)S(1)}, f32[2,384,2304]{2,1,0:T(8,128)}) fusion(f32[384,2304]{1,0:T(8,128)} %bitcast.170, bf16[384,2,64]{0,2,1:T(8,128)(2,1)S(1)} %bitcast.177, bf16[2304,2,64]{0,2,1:T(8,128)(2,1)S(1)} %bitcast.171), kind=kOutput, calls=%fused_computation.77.clone.1 | convolution fusion | flops 233572608 | bytes 11308032 | tf_op jit(solution)/shard_map/while/body/eval_jaxpr/sub | solution.py:103
  153.4 3.8 fusion.92
  157.3 1.2 fusion.93
  160.3 1.6 multiply_convert_fusion.2
  161.9 1.2 fusion.94
  165.2 1.6 constant_dynamic-update-slice_fusion.24
  166.7 6.4 %copy.25 = f32[2304,4,128]{2,1,0:T(4,128)} copy(f32[2304,4,128]{0,2,1:T(8,128)} %bitcast.185) | data formatting | bytes 9437184 | tf_op jit(solution)/shard_map/transpose | solution.py:56
  173.2 6.7 %concatenate.24 = f32[6,384,512]{2,1,0:T(8,128)} reshape(f32[2304,4,128]{2,1,0:T(4,128)} %copy.25) | data formatting | bytes 9437184 | tf_op jit(solution)/shard_map/concatenate | solution.py:131
  179.9 1.4 fusion.22
  181.3 2.0 convolution_bitcast_fusion.1
  183.2 6.5 %copy.24 = f32[2304,4,128]{2,1,0:T(4,128)} copy(f32[2304,4,128]{0,2,1:T(8,128)} %bitcast.186) | data formatting | bytes 9437184 | tf_op jit(solution)/shard_map/transpose | solution.py:56
  189.7 6.6 %concatenate.23 = f32[6,384,512]{2,1,0:T(8,128)} reshape(f32[2304,4,128]{2,1,0:T(4,128)} %copy.24) | data formatting | bytes 9437184 | tf_op jit(solution)/shard_map/concatenate | solution.py:131
  196.3 3.0 constant_dynamic-update-slice_fusion.12
  200.4 1.6 copy-done.16
  202.0 7.7 %convolution_bitcast_fusion = f32[512,1024]{1,0:T(8,128)S(1)} fusion(bf16[6,384,512]{2,1,0:T(8,128)(2,1)S(1)} %bitcast.196, f32[6,384,1024]{2,1,0:T(8,128)S(1)} %constant_dynamic-update-slice_fusion.11), kind=kOutput, calls=%fused_computation.28 | convolution fusion | flops 14495514624 | bytes 13893632 | tf_op jit(solution)/shard_map/scd,scf->df/dot_general | solution.py:139
  209.7 1.5 fusion.31
  211.2 10.5 %fusion.12 = f32[6,384,512]{2,1,0:T(8,128)S(1)} fusion(f32[6,384,1024]{2,1,0:T(8,128)} %copy-done.4, bf16[512,1024]{1,0:T(8,128)(2,1)S(1)} %copy-done.15), kind=kOutput, calls=%fused_computation.36 | convolution fusion | flops 14495514624 | bytes 15204352 | tf_op jit(solution)/shard_map/scf,df->scd/dot_general | solution.py:134
  223.1 1.3 collective-permute-start.7
  224.4 4.2 %collective-permute-start.6 = (f32[384,512]{1,0:T(8,128)S(1)}, f32[384,512]{1,0:T(8,128)S(1)}, u32[]{:S(2)}, u32[]{:S(2)}) collective-permute-start(f32[384,512]{1,0:T(8,128)S(1)} %get-tuple-element.140), channel_id=1, source_target_pairs={{1,0},{2,1},{3,2},{4,3},{5,4},{6,5},{7,6},{8,7},{9,8},{10,9},{11,1... | collective-permute-start | bytes 2359304 | tf_op jit(solution)/shard_map/ppermute | solution.py:23
  229.8 24.6 %collective-permute-done.5 = f32[384,512]{1,0:T(8,128)S(1)} collective-permute-done((f32[384,512]{1,0:T(8,128)S(1)}, f32[384,512]{1,0:T(8,128)S(1)}, u32[]{:S(2)}, u32[]{:S(2)}) %collective-permute-start.5) | collective-permute-done | bytes 786464 | tf_op jit(solution)/shard_map/ppermute | solution.py:20
  254.4 7.0 %collective-permute-done.9 = f32[384,512]{1,0:T(8,128)S(1)} collective-permute-done((f32[384,512]{1,0:T(8,128)S(1)}, f32[384,512]{1,0:T(8,128)S(1)}, u32[]{:S(2)}, u32[]{:S(2)}) %collective-permute-start.9) | collective-permute-done | bytes 786464 | tf_op jit(solution)/shard_map/ppermute | solution.py:31
  261.4 9.6 %collective-permute-done.8 = f32[384,512]{1,0:T(8,128)S(1)} collective-permute-done((f32[384,512]{1,0:T(8,128)S(1)}, f32[384,512]{1,0:T(8,128)S(1)}, u32[]{:S(2)}, u32[]{:S(2)}) %collective-permute-start.8) | collective-permute-done | bytes 786464 | tf_op jit(solution)/shard_map/ppermute | solution.py:31
  271.4 16.0 %collective-permute-done.6 = f32[384,512]{1,0:T(8,128)S(1)} collective-permute-done((f32[384,512]{1,0:T(8,128)S(1)}, f32[384,512]{1,0:T(8,128)S(1)}, u32[]{:S(2)}, u32[]{:S(2)}) %collective-permute-start.6) | collective-permute-done | bytes 786464 | tf_op jit(solution)/shard_map/ppermute | solution.py:23
  287.4 2.4 fusion.21
  289.8 111.5 %all-reduce.3.cloned.1.call-done = (f32[512,512]{0,1:T(8,128)}, f32[512,512]{1,0:T(8,128)}, f32[512,512]{1,0:T(8,128)}, f32[512,512]{1,0:T(8,128)}) async-done(((f32[512,512]{0,1:T(8,128)}, f32[512,512]{1,0:T(8,128)}, f32[512,512]{1,0:T(8,128)}, f32[512,512]{1,0:T(8,128)}), (f32[512,512]{0,1:T(8,128)}, f32[512,512]{1,0:T(8,128)}, f32[512,512]{1,0:T(8,128)}, ...) | async-done | bytes 4194320 | tf_op jit(solution)/shard_map/psum | solution.py:143
  401.2 2.7 copy.27
  403.9 2.3 copy.89
  (141 shorter events, 41.0 us)
Async XLA Ops:
  7.2 15.5 %copy-start = (bf16[512,512]{1,0:T(8,128)(2,1)S(1)}, bf16[512,512]{1,0:T(8,128)(2,1)}, u32[]{:S(2)}) copy-start(bf16[512,512]{1,0:T(8,128)(2,1)} %param.15) | copy-start | bytes 1572868
  7.2 14.9 %copy-start.2 = (bf16[1,384,512]{2,1,0:T(8,128)(2,1)S(1)}, bf16[1,384,512]{2,1,0:T(8,128)(2,1)}, u32[]{:S(2)}) copy-start(bf16[1,384,512]{2,1,0:T(8,128)(2,1)} %param.9) | copy-start | bytes 1179652
  7.2 15.5 %copy-start.8 = (bf16[1,384,512]{2,1,0:T(8,128)(2,1)S(1)}, bf16[1,384,512]{2,1,0:T(8,128)(2,1)}, u32[]{:S(2)}) copy-start(bf16[1,384,512]{2,1,0:T(8,128)(2,1)} %param.11) | copy-start | bytes 1179652
  7.2 394.0 %all-reduce.3.cloned.1.call-start = ((), (), s32[]{:S(2)}) async-start(), calls=%async_computation | async-start | bytes 8388608 | tf_op jit(solution)/shard_map/psum | solution.py:143
  7.2 39.0 %collective-permute-start.3 = (bf16[384,512]{1,0:T(8,128)(2,1)}, bf16[384,512]{1,0:T(8,128)(2,1)}, u32[]{:S(2)}, u32[]{:S(2)}) collective-permute-start(bf16[384,512]{1,0:T(8,128)(2,1)} %bitcast.187), channel_id=1, source_target_pairs={{0,4},{1,5},{2,6},{3,7},{4,0},{5,1},{6,2},{7,3},{8,12},{9,13},{10,... | collective-permute-start | bytes 1179656 | tf_op jit(solution)/shard_map/ppermute | solution.py:31
  10.4 34.1 %collective-permute-start.2 = (bf16[384,512]{1,0:T(8,128)(2,1)}, bf16[384,512]{1,0:T(8,128)(2,1)}, u32[]{:S(2)}, u32[]{:S(2)}) collective-permute-start(bf16[384,512]{1,0:T(8,128)(2,1)} %bitcast.188), channel_id=1, source_target_pairs={{0,8},{1,9},{2,10},{3,11},{4,12},{5,13},{6,14},{7,15},{8,0},{9,1},... | collective-permute-start | bytes 1179656 | tf_op jit(solution)/shard_map/ppermute | solution.py:31
  13.0 29.7 %collective-permute-start.1 = (bf16[384,512]{1,0:T(8,128)(2,1)}, bf16[384,512]{1,0:T(8,128)(2,1)}, u32[]{:S(2)}, u32[]{:S(2)}) collective-permute-start(bf16[384,512]{1,0:T(8,128)(2,1)} %bitcast.189), channel_id=1, source_target_pairs={{1,0},{2,1},{3,2},{4,3},{5,4},{6,5},{7,6},{8,7},{9,8},{10,9},{11,1... | collective-permute-start | bytes 1179656 | tf_op jit(solution)/shard_map/ppermute | solution.py:23
  15.1 25.8 %collective-permute-start = (bf16[384,512]{1,0:T(8,128)(2,1)}, bf16[384,512]{1,0:T(8,128)(2,1)}, u32[]{:S(2)}, u32[]{:S(2)}) collective-permute-start(bf16[384,512]{1,0:T(8,128)(2,1)} %bitcast.190), channel_id=1, source_target_pairs={{0,1},{1,2},{2,3},{3,4},{4,5},{5,6},{6,7},{7,8},{8,9},{9,10},{10,1... | collective-permute-start | bytes 1179656 | tf_op jit(solution)/shard_map/ppermute | solution.py:20
  15.1 33.0 %collective-permute-start.4 = (bf16[384,512]{1,0:T(8,128)(2,1)}, bf16[384,512]{1,0:T(8,128)(2,1)}, u32[]{:S(2)}, u32[]{:S(2)}) collective-permute-start(bf16[384,512]{1,0:T(8,128)(2,1)} %bitcast.191), channel_id=1, source_target_pairs={{0,2},{1,3},{2,0},{3,1},{4,6},{5,7},{6,4},{7,5},{8,10},{9,11},{10,... | collective-permute-start | bytes 1179656 | tf_op jit(solution)/shard_map/ppermute | solution.py:31
  18.3 4.8 %copy-start.17 = (s32[1,3,18]{2,0,1:T(1,128)S(1)}, s32[1,3,18]{2,0,1:T(1,128)}, u32[]{:S(2)}) copy-start(s32[1,3,18]{2,0,1:T(1,128)} %param.10) | copy-start | bytes 652
  22.1 1.0 copy-start.13
  23.2 26.7 %copy-start.14 = (bf16[512,1024]{1,0:T(8,128)(2,1)S(1)}, bf16[512,1024]{1,0:T(8,128)(2,1)}, u32[]{:S(2)}) copy-start(bf16[512,1024]{1,0:T(8,128)(2,1)} %copy-done.13) | copy-start | bytes 3145732
  55.9 1.5 copy-start.6
  74.1 3.0 copy-start.1
  80.7 3.0 copy-start.7
  83.7 1.5 copy-start.6
  101.9 3.0 copy-start.1
  108.5 3.0 copy-start.7
  111.4 1.5 copy-start.6
  129.6 3.0 copy-start.1
  136.2 2.9 copy-start.7
  139.1 1.5 copy-start.6
  157.2 3.0 copy-start.1
  163.8 2.9 copy-start.7
  173.2 6.7 %copy-start.9 = (bf16[1,384,512]{2,1,0:T(8,128)(2,1)S(1)}, bf16[1,384,512]{2,1,0:T(8,128)(2,1)}, u32[]{:S(2)}) copy-start(bf16[1,384,512]{2,1,0:T(8,128)(2,1)} %param.11) | copy-start | bytes 1179652
  173.2 6.7 %copy-start.10 = (bf16[4,384,128]{1,2,0:T(8,128)(2,1)S(1)}, bf16[4,384,128]{1,2,0:T(8,128)(2,1)}, u32[]{:S(2)}) copy-start(bf16[4,384,128]{1,2,0:T(8,128)(2,1)} %get-tuple-element.66) | copy-start | bytes 1179652
  173.2 8.1 %copy-start.3 = (f32[4,384,128]{1,2,0:T(8,128)S(1)}, f32[4,384,128]{1,2,0:T(8,128)}, u32[]{:S(2)}) copy-start(f32[4,384,128]{1,2,0:T(8,128)} %get-tuple-element.67) | copy-start | bytes 2359300
  189.7 9.6 %slice-start = ((s8[4718592]{0:T(1024)(128)(4,1)}), s8[524288]{0:T(1024)(128)(4,1)S(1)}, s32[]{:S(2)}) async-start(s8[4718592]{0:T(1024)(128)(4,1)} %bitcast.182), calls=%async_computation.1 | async-start | bytes 1048576
  196.3 3.6 slice-start.1
  199.9 2.1 copy-start.16
  200.4 9.3 %copy-start.4 = (f32[6,384,1024]{2,1,0:T(8,128)}, f32[6,384,1024]{2,1,0:T(8,128)S(1)}, u32[]{:S(2)}) copy-start(f32[6,384,1024]{2,1,0:T(8,128)S(1)} %constant_dynamic-update-slice_fusion.11) | copy-start | bytes 28311556
  209.7 1.5 copy-start.15
  221.7 65.7 %copy-start.5 = (bf16[512,512]{1,0:T(8,128)(2,1)S(1)}, bf16[512,512]{1,0:T(8,128)(2,1)}, u32[]{:S(2)}) copy-start(bf16[512,512]{1,0:T(8,128)(2,1)} %param.12) | copy-start | bytes 1572868
  222.2 32.2 %collective-permute-start.5 = (f32[384,512]{1,0:T(8,128)S(1)}, f32[384,512]{1,0:T(8,128)S(1)}, u32[]{:S(2)}, u32[]{:S(2)}) collective-permute-start(f32[384,512]{1,0:T(8,128)S(1)} %get-tuple-element.136), channel_id=1, source_target_pairs={{0,1},{1,2},{2,3},{3,4},{4,5},{5,6},{6,7},{7,8},{8,9},{9,10},{10,1... | collective-permute-start | bytes 2359304 | tf_op jit(solution)/shard_map/ppermute | solution.py:20
  222.2 39.2 %collective-permute-start.9 = (f32[384,512]{1,0:T(8,128)S(1)}, f32[384,512]{1,0:T(8,128)S(1)}, u32[]{:S(2)}, u32[]{:S(2)}) collective-permute-start(f32[384,512]{1,0:T(8,128)S(1)} %get-tuple-element.137), channel_id=1, source_target_pairs={{0,2},{1,3},{2,0},{3,1},{4,6},{5,7},{6,4},{7,5},{8,10},{9,11},{10,... | collective-permute-start | bytes 2359304 | tf_op jit(solution)/shard_map/ppermute | solution.py:31
  222.3 48.7 %collective-permute-start.8 = (f32[384,512]{1,0:T(8,128)S(1)}, f32[384,512]{1,0:T(8,128)S(1)}, u32[]{:S(2)}, u32[]{:S(2)}) collective-permute-start(f32[384,512]{1,0:T(8,128)S(1)} %get-tuple-element.138), channel_id=1, source_target_pairs={{0,4},{1,5},{2,6},{3,7},{4,0},{5,1},{6,2},{7,3},{8,12},{9,13},{10,... | collective-permute-start | bytes 2359304 | tf_op jit(solution)/shard_map/ppermute | solution.py:31
  223.1 48.3 %collective-permute-start.7 = (f32[384,512]{1,0:T(8,128)S(1)}, f32[384,512]{1,0:T(8,128)S(1)}, u32[]{:S(2)}, u32[]{:S(2)}) collective-permute-start(f32[384,512]{1,0:T(8,128)S(1)} %get-tuple-element.139), channel_id=1, source_target_pairs={{0,8},{1,9},{2,10},{3,11},{4,12},{5,13},{6,14},{7,15},{8,0},{9,1},... | collective-permute-start | bytes 2359304 | tf_op jit(solution)/shard_map/ppermute | solution.py:31
  224.4 63.0 %collective-permute-start.6 = (f32[384,512]{1,0:T(8,128)S(1)}, f32[384,512]{1,0:T(8,128)S(1)}, u32[]{:S(2)}, u32[]{:S(2)}) collective-permute-start(f32[384,512]{1,0:T(8,128)S(1)} %get-tuple-element.140), channel_id=1, source_target_pairs={{1,0},{2,1},{3,2},{4,3},{5,4},{6,5},{7,6},{8,7},{9,8},{10,9},{11,1... | collective-permute-start | bytes 2359304 | tf_op jit(solution)/shard_map/ppermute | solution.py:23
  401.2 4.9 %copy-start.12 = (f32[512,512]{1,0:T(8,128)S(1)}, f32[512,512]{1,0:T(8,128)}, u32[]{:S(2)}) copy-start(f32[512,512]{1,0:T(8,128)} %get-tuple-element.283) | copy-start | bytes 3145732
  401.2 5.9 %copy-start.11 = (f32[512,512]{1,0:T(8,128)S(1)}, f32[512,512]{1,0:T(8,128)}, u32[]{:S(2)}) copy-start(f32[512,512]{1,0:T(8,128)} %get-tuple-element.284) | copy-start | bytes 3145732
Sparse Core Ops, SparseCore 0:
  211.3 189.8 all-reduce.2
where the time goes:
time: 417 us; the launch traced here: 415 us
  waiting for transfers between devices  187 us (45%)
  local copies, waits for them, and re-layouts  95.9 us (23%)
  matrix products  80.1 us (19%)
  other arithmetic  19.1 us (5%)
  starting transfers between devices  15.7 us (4%)
  between operations  14.3 us (3%)
    psum x1, waiting for transfers between devices, per_device(): lax.psum((g_query, g_both[:, :width_all], g_both[:, width_all:], g_out),...  111 us
    ppermute x2, waiting for transfers between devices, with_halo(): lax.ppermute(lax.slice_in_dim(block, block.shape[dim] - width, None, axis...  42.2 us
    sub x4, matrix products, head_pair(): exp_vals = jnp.exp(scores - row_max)  28.4 us
    unnamed x45, local copies, waits for them, and re-layouts  22.3 us
    ppermute x6, waiting for transfers between devices, from_partner(): return lax.ppermute(value, axis, pairs)  17 us
    ppermute x2, waiting for transfers between devices, with_halo(): lax.ppermute(lax.slice_in_dim(block, 0, width, axis=dim), axis, backward)  16 us
    convert_element_type x4, other arithmetic, head_pair(): prob_bf = prob_f32.astype(jnp.bfloat16)  15.3 us
    while x28, local copies, waits for them, and re-layouts  14.3 us
  transfers between devices with their start and end apart: 11, of which 7 were waited for; matrix products, arithmetic and copies ran while one was open for 7% of the time, Pallas kernels for 0%

commit v1 on v0

--- a/solution.py
+++ b/solution.py
@@ -9,6 +9,11 @@
 TILE_DEV = 3
 NB = 3
 CANDT = 18
+
+
+def by_each_axis(x, one, other):
+    inner = lax.psum(x, one)
+    return lax.psum(inner, other)
 
 
 def with_halo(block, sides, width):
@@ -140,8 +145,8 @@
     grad_x = jnp.dot(grad_q, w_query.astype(jnp.float32).T, precision=highest) + kv_dx
     g_query = jnp.dot(rows_f32.T, grad_q, precision=highest)
     g_out = jnp.dot(out_rows.T, cot_rows, preferred_element_type=jnp.float32)
-    g_query, g_key, g_value, g_out = lax.psum(
-        (g_query, g_both[:, :width_all], g_both[:, width_all:], g_out), ("dp", "dom")
+    g_query, g_key, g_value, g_out = by_each_axis(
+        (g_query, g_both[:, :width_all], g_both[:, width_all:], g_out), "dom", "dp"
     )
     return (attended[None], grad_x.astype(jnp.bfloat16)[None], g_query, g_key, g_value, g_out)
 

time: 417 us -> 460 us (1.10)
  waiting for transfers between devices: 187 us -> 227 us
    psum x1 -> x2, waiting for transfers between devices: 111 us -> 166 us  [the longest x1 166 us: by_each_axis(): inner = lax.psum(x, one)]
    ppermute x2, waiting for transfers between devices: 42.2 us -> 32.4 us  [with_halo(): lax.ppermute(lax.slice_in_dim(block, block.shape[dim] - width, None, axis...]
    ppermute x2, waiting for transfers between devices: 16 us -> 11.4 us  [with_halo(): lax.ppermute(lax.slice_in_dim(block, 0, width, axis=dim), axis, backward)]
  transfers between devices with their start and end apart: 11 -> 12, of which waited for: 7 -> 7; matrix products, arithmetic and copies ran while one was open for 7% -> 6% of each run, Pallas kernels for 0% -> 0%
where the time goes in v1:
time: 460 us; the launch traced here: 457 us
  waiting for transfers between devices  227 us (49%)
  local copies, waits for them, and re-layouts  95.9 us (21%)
  matrix products  80 us (17%)
  other arithmetic  19.1 us (4%)
  starting transfers between devices  17.6 us (4%)
  between operations  14.3 us (3%)
    psum x1, waiting for transfers between devices, by_each_axis(): inner = lax.psum(x, one)  166 us
    ppermute x2, waiting for transfers between devices, with_halo(): lax.ppermute(lax.slice_in_dim(block, block.shape[dim] - width, None, axis...  32.4 us
    sub x4, matrix products, head_pair(): exp_vals = jnp.exp(scores - row_max)  28.3 us
    unnamed x45, local copies, waits for them, and re-layouts  22.3 us
    ppermute x6, waiting for transfers between devices, from_partner(): return lax.ppermute(value, axis, pairs)  17.4 us
    convert_element_type x4, other arithmetic, head_pair(): prob_bf = prob_f32.astype(jnp.bfloat16)  15.3 us
    while x28, local copies, waits for them, and re-layouts  14.3 us
    concatenate x3, local copies, waits for them, and re-layouts, per_device(): jnp.concatenate([grad_k, grad_v], 1)  13.7 us
  transfers between devices with their start and end apart: 12, of which 7 were waited for; matrix products, arithmetic and copies ran while one was open for 6% of the time, Pallas kernels for 0%

profile of v1, /device:TPU:0, one launch (start us, length us, event | category | flops | bytes accessed | tf_op | source)
XLA Modules:
  0.0 457.1 jit_solution(3954026942510519333)
XLA Ops:
  7.2 3.1 collective-permute-start.3
  10.4 2.6 collective-permute-start.2
  13.0 2.1 collective-permute-start.1
  15.1 1.4 collective-permute-start.4
  16.5 1.8 constant_dynamic-update-slice_fusion.18
  18.3 1.5 convolution_convert_fusion.5
  23.2 17.6 %collective-permute-done = bf16[384,512]{1,0:T(8,128)(2,1)} collective-permute-done((bf16[384,512]{1,0:T(8,128)(2,1)}, bf16[384,512]{1,0:T(8,128)(2,1)}, u32[]{:S(2)}, u32[]{:S(2)}) %collective-permute-start) | collective-permute-done | bytes 393248 | tf_op jit(solution)/shard_map/ppermute | solution.py:25
  40.8 1.8 constant_dynamic-update-slice_fusion.17
  42.7 1.8 constant_dynamic-update-slice_fusion.16
  44.5 1.8 constant_dynamic-update-slice_fusion.15
  46.3 1.8 constant_dynamic-update-slice_fusion.14
  48.1 1.8 constant_dynamic-update-slice_fusion.13
  49.9 2.2 convolution_convert_fusion.1
  52.1 3.8 pad_maximum_fusion
  56.0 110.7 %while.16 = (s32[]{:T(128)}, bf16[4,384,128]{1,2,0:T(8,128)(2,1)}, f32[4,384,128]{1,2,0:T(8,128)}, f32[4,2304,128]{1,2,0:T(8,128)}, f32[4,2304,128]{1,2,0:T(8,12...) while((s32[]{:T(128)}, bf16[4,384,128]{1,2,0:T(8,128)(2,1)}, ...), condition=%wide.region_3.4_spmd, body=%wide.region_0.3_spmd.sunk | while | flops 1378665984 | bytes 104414744 | solution.py:130
  60.7 2.5 copy.52
  63.2 7.1 %fusion.91 = (f32[2,384]{1,0:T(2,128)S(1)}, f32[2,384,2304]{2,1,0:T(8,128)}) fusion(f32[384,2304]{1,0:T(8,128)} %bitcast.170, bf16[384,2,64]{0,2,1:T(8,128)(2,1)S(1)} %bitcast.177, bf16[2304,2,64]{0,2,1:T(8,128)(2,1)S(1)} %bitcast.171), kind=kOutput, calls=%fused_computation.77.clone.1 | convolution fusion | flops 233572608 | bytes 11308032 | tf_op jit(solution)/shard_map/while/body/eval_jaxpr/sub | solution.py:108
  70.3 3.8 fusion.92
  74.1 1.2 fusion.93
  77.1 1.6 multiply_convert_fusion.2
  82.0 1.7 constant_dynamic-update-slice_fusion.24
  88.4 2.5 copy.52
  90.9 7.1 %fusion.91 = (f32[2,384]{1,0:T(2,128)S(1)}, f32[2,384,2304]{2,1,0:T(8,128)}) fusion(f32[384,2304]{1,0:T(8,128)} %bitcast.170, bf16[384,2,64]{0,2,1:T(8,128)(2,1)S(1)} %bitcast.177, bf16[2304,2,64]{0,2,1:T(8,128)(2,1)S(1)} %bitcast.171), kind=kOutput, calls=%fused_computation.77.clone.1 | convolution fusion | flops 233572608 | bytes 11308032 | tf_op jit(solution)/shard_map/while/body/eval_jaxpr/sub | solution.py:108
  98.0 3.8 fusion.92
  101.9 1.2 fusion.93
  104.9 1.6 multiply_convert_fusion.2
  109.8 1.6 constant_dynamic-update-slice_fusion.24
  116.1 2.5 copy.52
  118.6 7.1 %fusion.91 = (f32[2,384]{1,0:T(2,128)S(1)}, f32[2,384,2304]{2,1,0:T(8,128)}) fusion(f32[384,2304]{1,0:T(8,128)} %bitcast.170, bf16[384,2,64]{0,2,1:T(8,128)(2,1)S(1)} %bitcast.177, bf16[2304,2,64]{0,2,1:T(8,128)(2,1)S(1)} %bitcast.171), kind=kOutput, calls=%fused_computation.77.clone.1 | convolution fusion | flops 233572608 | bytes 11308032 | tf_op jit(solution)/shard_map/while/body/eval_jaxpr/sub | solution.py:108
  125.7 3.8 fusion.92
  129.5 1.2 fusion.93
  132.5 1.6 multiply_convert_fusion.2
  137.5 1.6 constant_dynamic-update-slice_fusion.24
  143.8 2.5 copy.52
  146.3 7.1 %fusion.91 = (f32[2,384]{1,0:T(2,128)S(1)}, f32[2,384,2304]{2,1,0:T(8,128)}) fusion(f32[384,2304]{1,0:T(8,128)} %bitcast.170, bf16[384,2,64]{0,2,1:T(8,128)(2,1)S(1)} %bitcast.177, bf16[2304,2,64]{0,2,1:T(8,128)(2,1)S(1)} %bitcast.171), kind=kOutput, calls=%fused_computation.77.clone.1 | convolution fusion | flops 233572608 | bytes 11308032 | tf_op jit(solution)/shard_map/while/body/eval_jaxpr/sub | solution.py:108
  153.4 3.8 fusion.92
  157.2 1.2 fusion.93
  160.2 1.6 multiply_convert_fusion.2
  161.8 1.2 fusion.94
  165.1 1.6 constant_dynamic-update-slice_fusion.24
  166.7 6.5 %copy.25 = f32[2304,4,128]{2,1,0:T(4,128)} copy(f32[2304,4,128]{0,2,1:T(8,128)} %bitcast.185) | data formatting | bytes 9437184 | tf_op jit(solution)/shard_map/transpose | solution.py:61
  173.2 6.6 %concatenate.24 = f32[6,384,512]{2,1,0:T(8,128)} reshape(f32[2304,4,128]{2,1,0:T(4,128)} %copy.25) | data formatting | bytes 9437184 | tf_op jit(solution)/shard_map/concatenate | solution.py:136
  179.8 1.4 fusion.22
  181.2 2.0 convolution_bitcast_fusion.1
  183.2 6.4 %copy.24 = f32[2304,4,128]{2,1,0:T(4,128)} copy(f32[2304,4,128]{0,2,1:T(8,128)} %bitcast.186) | data formatting | bytes 9437184 | tf_op jit(solution)/shard_map/transpose | solution.py:61
  189.6 6.6 %concatenate.23 = f32[6,384,512]{2,1,0:T(8,128)} reshape(f32[2304,4,128]{2,1,0:T(4,128)} %copy.24) | data formatting | bytes 9437184 | tf_op jit(solution)/shard_map/concatenate | solution.py:136
  196.2 3.0 constant_dynamic-update-slice_fusion.12
  200.3 1.6 copy-done.16
  201.9 7.7 %convolution_bitcast_fusion = f32[512,1024]{1,0:T(8,128)S(1)} fusion(bf16[6,384,512]{2,1,0:T(8,128)(2,1)S(1)} %bitcast.196, f32[6,384,1024]{2,1,0:T(8,128)S(1)} %constant_dynamic-update-slice_fusion.11), kind=kOutput, calls=%fused_computation.28 | convolution fusion | flops 14495514624 | bytes 13893632 | tf_op jit(solution)/shard_map/scd,scf->df/dot_general | solution.py:144
  209.6 1.5 fusion.31
  211.2 165.9 %all-reduce.5.cloned.1.call-done = (f32[512,512]{0,1:T(8,128)}, f32[512,512]{1,0:T(8,128)}, f32[512,512]{1,0:T(8,128)}, f32[512,512]{1,0:T(8,128)}) async-done(((f32[512,512]{0,1:T(8,128)}, f32[512,512]{1,0:T(8,128)}, f32[512,512]{1,0:T(8,128)}, f32[512,512]{1,0:T(8,128)}), (f32[512,512]{0,1:T(8,128)}, f32[512,512]{1,0:T(8,128)}, f32[512,512]{1,0:T(8,128)}, ...) | async-done | bytes 4194320 | tf_op jit(solution)/shard_map/psum | solution.py:15
  377.2 10.5 %fusion.12 = f32[6,384,512]{2,1,0:T(8,128)S(1)} fusion(f32[6,384,1024]{2,1,0:T(8,128)} %copy-done.4, bf16[512,1024]{1,0:T(8,128)(2,1)S(1)} %copy-done.15), kind=kOutput, calls=%fused_computation.36 | convolution fusion | flops 14495514624 | bytes 15204352 | tf_op jit(solution)/shard_map/scf,df->scd/dot_general | solution.py:139
  388.1 1.5 collective-permute-start.5
  389.6 1.5 collective-permute-start.9
  391.5 1.6 collective-permute-start.7
  393.0 3.3 collective-permute-start.6
  397.5 14.8 %collective-permute-done.5 = f32[384,512]{1,0:T(8,128)S(1)} collective-permute-done((f32[384,512]{1,0:T(8,128)S(1)}, f32[384,512]{1,0:T(8,128)S(1)}, u32[]{:S(2)}, u32[]{:S(2)}) %collective-permute-start.5) | collective-permute-done | bytes 786464 | tf_op jit(solution)/shard_map/ppermute | solution.py:25
  412.3 12.8 %collective-permute-done.9 = f32[384,512]{1,0:T(8,128)S(1)} collective-permute-done((f32[384,512]{1,0:T(8,128)S(1)}, f32[384,512]{1,0:T(8,128)S(1)}, u32[]{:S(2)}, u32[]{:S(2)}) %collective-permute-start.9) | collective-permute-done | bytes 786464 | tf_op jit(solution)/shard_map/ppermute | solution.py:36
  425.1 1.3 collective-permute-done.8
  426.4 3.2 collective-permute-done.7
  429.7 11.4 %collective-permute-done.6 = f32[384,512]{1,0:T(8,128)S(1)} collective-permute-done((f32[384,512]{1,0:T(8,128)S(1)}, f32[384,512]{1,0:T(8,128)S(1)}, u32[]{:S(2)}, u32[]{:S(2)}) %collective-permute-start.6) | collective-permute-done | bytes 786464 | tf_op jit(solution)/shard_map/ppermute | solution.py:28
  441.0 2.4 fusion.21
  443.4 2.7 copy.27
  446.1 2.3 copy.93
  (144 shorter events, 43.6 us)
Async XLA Ops:
  7.2 15.5 %copy-start = (bf16[512,512]{1,0:T(8,128)(2,1)S(1)}, bf16[512,512]{1,0:T(8,128)(2,1)}, u32[]{:S(2)}) copy-start(bf16[512,512]{1,0:T(8,128)(2,1)} %param.15) | copy-start | bytes 1572868
  7.2 14.9 %copy-start.2 = (bf16[1,384,512]{2,1,0:T(8,128)(2,1)S(1)}, bf16[1,384,512]{2,1,0:T(8,128)(2,1)}, u32[]{:S(2)}) copy-start(bf16[1,384,512]{2,1,0:T(8,128)(2,1)} %param.9) | copy-start | bytes 1179652
  7.2 15.5 %copy-start.8 = (bf16[1,384,512]{2,1,0:T(8,128)(2,1)S(1)}, bf16[1,384,512]{2,1,0:T(8,128)(2,1)}, u32[]{:S(2)}) copy-start(bf16[1,384,512]{2,1,0:T(8,128)(2,1)} %param.11) | copy-start | bytes 1179652
  7.2 369.9 %all-reduce.5.cloned.1.call-start = ((), (), s32[]{:S(2)}) async-start(), calls=%async_computation | async-start | bytes 8388608 | tf_op jit(solution)/shard_map/psum | solution.py:15
  7.2 39.0 %collective-permute-start.3 = (bf16[384,512]{1,0:T(8,128)(2,1)}, bf16[384,512]{1,0:T(8,128)(2,1)}, u32[]{:S(2)}, u32[]{:S(2)}) collective-permute-start(bf16[384,512]{1,0:T(8,128)(2,1)} %bitcast.187), channel_id=1, source_target_pairs={{0,4},{1,5},{2,6},{3,7},{4,0},{5,1},{6,2},{7,3},{8,12},{9,13},{10,... | collective-permute-start | bytes 1179656 | tf_op jit(solution)/shard_map/ppermute | solution.py:36
  10.4 34.1 %collective-permute-start.2 = (bf16[384,512]{1,0:T(8,128)(2,1)}, bf16[384,512]{1,0:T(8,128)(2,1)}, u32[]{:S(2)}, u32[]{:S(2)}) collective-permute-start(bf16[384,512]{1,0:T(8,128)(2,1)} %bitcast.188), channel_id=1, source_target_pairs={{0,8},{1,9},{2,10},{3,11},{4,12},{5,13},{6,14},{7,15},{8,0},{9,1},... | collective-permute-start | bytes 1179656 | tf_op jit(solution)/shard_map/ppermute | solution.py:36
  13.0 29.7 %collective-permute-start.1 = (bf16[384,512]{1,0:T(8,128)(2,1)}, bf16[384,512]{1,0:T(8,128)(2,1)}, u32[]{:S(2)}, u32[]{:S(2)}) collective-permute-start(bf16[384,512]{1,0:T(8,128)(2,1)} %bitcast.189), channel_id=1, source_target_pairs={{1,0},{2,1},{3,2},{4,3},{5,4},{6,5},{7,6},{8,7},{9,8},{10,9},{11,1... | collective-permute-start | bytes 1179656 | tf_op jit(solution)/shard_map/ppermute | solution.py:28
  15.1 25.8 %collective-permute-start = (bf16[384,512]{1,0:T(8,128)(2,1)}, bf16[384,512]{1,0:T(8,128)(2,1)}, u32[]{:S(2)}, u32[]{:S(2)}) collective-permute-start(bf16[384,512]{1,0:T(8,128)(2,1)} %bitcast.190), channel_id=1, source_target_pairs={{0,1},{1,2},{2,3},{3,4},{4,5},{5,6},{6,7},{7,8},{8,9},{9,10},{10,1... | collective-permute-start | bytes 1179656 | tf_op jit(solution)/shard_map/ppermute | solution.py:25
  15.1 33.0 %collective-permute-start.4 = (bf16[384,512]{1,0:T(8,128)(2,1)}, bf16[384,512]{1,0:T(8,128)(2,1)}, u32[]{:S(2)}, u32[]{:S(2)}) collective-permute-start(bf16[384,512]{1,0:T(8,128)(2,1)} %bitcast.191), channel_id=1, source_target_pairs={{0,2},{1,3},{2,0},{3,1},{4,6},{5,7},{6,4},{7,5},{8,10},{9,11},{10,... | collective-permute-start | bytes 1179656 | tf_op jit(solution)/shard_map/ppermute | solution.py:36
  18.3 4.8 %copy-start.17 = (s32[1,3,18]{2,0,1:T(1,128)S(1)}, s32[1,3,18]{2,0,1:T(1,128)}, u32[]{:S(2)}) copy-start(s32[1,3,18]{2,0,1:T(1,128)} %param.10) | copy-start | bytes 652
  22.1 1.0 copy-start.13
  23.2 26.7 %copy-start.14 = (bf16[512,1024]{1,0:T(8,128)(2,1)S(1)}, bf16[512,1024]{1,0:T(8,128)(2,1)}, u32[]{:S(2)}) copy-start(bf16[512,1024]{1,0:T(8,128)(2,1)} %copy-done.13) | copy-start | bytes 3145732
  56.0 1.5 copy-start.6
  74.1 3.0 copy-start.1
  80.7 3.0 copy-start.7
  83.7 1.5 copy-start.6
  101.8 3.0 copy-start.1
  108.4 3.0 copy-start.7
  111.4 1.5 copy-start.6
  129.5 3.0 copy-start.1
  136.1 2.9 copy-start.7
  139.1 1.5 copy-start.6
  157.2 3.0 copy-start.1
  163.8 2.9 copy-start.7
  173.1 6.7 %copy-start.9 = (bf16[1,384,512]{2,1,0:T(8,128)(2,1)S(1)}, bf16[1,384,512]{2,1,0:T(8,128)(2,1)}, u32[]{:S(2)}) copy-start(bf16[1,384,512]{2,1,0:T(8,128)(2,1)} %param.11) | copy-start | bytes 1179652
  173.1 6.7 %copy-start.10 = (bf16[4,384,128]{1,2,0:T(8,128)(2,1)S(1)}, bf16[4,384,128]{1,2,0:T(8,128)(2,1)}, u32[]{:S(2)}) copy-start(bf16[4,384,128]{1,2,0:T(8,128)(2,1)} %get-tuple-element.66) | copy-start | bytes 1179652
  173.1 8.1 %copy-start.3 = (f32[4,384,128]{1,2,0:T(8,128)S(1)}, f32[4,384,128]{1,2,0:T(8,128)}, u32[]{:S(2)}) copy-start(f32[4,384,128]{1,2,0:T(8,128)} %get-tuple-element.67) | copy-start | bytes 2359300
  189.6 9.6 %slice-start = ((s8[4718592]{0:T(1024)(128)(4,1)}), s8[524288]{0:T(1024)(128)(4,1)S(1)}, s32[]{:S(2)}) async-start(s8[4718592]{0:T(1024)(128)(4,1)} %bitcast.182), calls=%async_computation.2 | async-start | bytes 1048576
  196.2 3.6 slice-start.1
  199.8 2.1 copy-start.16
  200.3 9.3 %copy-start.4 = (f32[6,384,1024]{2,1,0:T(8,128)}, f32[6,384,1024]{2,1,0:T(8,128)S(1)}, u32[]{:S(2)}) copy-start(f32[6,384,1024]{2,1,0:T(8,128)S(1)} %constant_dynamic-update-slice_fusion.11) | copy-start | bytes 28311556
  211.1 166.0 %copy-start.15 = (bf16[512,1024]{1,0:T(8,128)(2,1)S(1)}, bf16[512,1024]{1,0:T(8,128)(2,1)}, u32[]{:S(2)}) copy-start(bf16[512,1024]{1,0:T(8,128)(2,1)} %copy-done.13) | copy-start | bytes 3145732
  211.2 232.2 %all-reduce.7.cloned.1.call-start = ((), (), s32[]{:S(2)}) async-start(), calls=%async_computation.1 | async-start | bytes 8388608 | tf_op jit(solution)/shard_map/psum | solution.py:16
  387.7 53.4 %copy-start.5 = (bf16[512,512]{1,0:T(8,128)(2,1)S(1)}, bf16[512,512]{1,0:T(8,128)(2,1)}, u32[]{:S(2)}) copy-start(bf16[512,512]{1,0:T(8,128)(2,1)} %param.12) | copy-start | bytes 1572868
  388.1 24.2 %collective-permute-start.5 = (f32[384,512]{1,0:T(8,128)S(1)}, f32[384,512]{1,0:T(8,128)S(1)}, u32[]{:S(2)}, u32[]{:S(2)}) collective-permute-start(f32[384,512]{1,0:T(8,128)S(1)} %get-tuple-element.140), channel_id=1, source_target_pairs={{0,1},{1,2},{2,3},{3,4},{4,5},{5,6},{6,7},{7,8},{8,9},{9,10},{10,1... | collective-permute-start | bytes 2359304 | tf_op jit(solution)/shard_map/ppermute | solution.py:25
  389.6 35.5 %collective-permute-start.9 = (f32[384,512]{1,0:T(8,128)S(1)}, f32[384,512]{1,0:T(8,128)S(1)}, u32[]{:S(2)}, u32[]{:S(2)}) collective-permute-start(f32[384,512]{1,0:T(8,128)S(1)} %get-tuple-element.141), channel_id=1, source_target_pairs={{0,2},{1,3},{2,0},{3,1},{4,6},{5,7},{6,4},{7,5},{8,10},{9,11},{10,... | collective-permute-start | bytes 2359304 | tf_op jit(solution)/shard_map/ppermute | solution.py:36
  391.1 35.3 %collective-permute-start.8 = (f32[384,512]{1,0:T(8,128)S(1)}, f32[384,512]{1,0:T(8,128)S(1)}, u32[]{:S(2)}, u32[]{:S(2)}) collective-permute-start(f32[384,512]{1,0:T(8,128)S(1)} %get-tuple-element.142), channel_id=1, source_target_pairs={{0,4},{1,5},{2,6},{3,7},{4,0},{5,1},{6,2},{7,3},{8,12},{9,13},{10,... | collective-permute-start | bytes 2359304 | tf_op jit(solution)/shard_map/ppermute | solution.py:36
  391.5 38.2 %collective-permute-start.7 = (f32[384,512]{1,0:T(8,128)S(1)}, f32[384,512]{1,0:T(8,128)S(1)}, u32[]{:S(2)}, u32[]{:S(2)}) collective-permute-start(f32[384,512]{1,0:T(8,128)S(1)} %get-tuple-element.143), channel_id=1, source_target_pairs={{0,8},{1,9},{2,10},{3,11},{4,12},{5,13},{6,14},{7,15},{8,0},{9,1},... | collective-permute-start | bytes 2359304 | tf_op jit(solution)/shard_map/ppermute | solution.py:36
  393.0 48.0 %collective-permute-start.6 = (f32[384,512]{1,0:T(8,128)S(1)}, f32[384,512]{1,0:T(8,128)S(1)}, u32[]{:S(2)}, u32[]{:S(2)}) collective-permute-start(f32[384,512]{1,0:T(8,128)S(1)} %get-tuple-element.144), channel_id=1, source_target_pairs={{1,0},{2,1},{3,2},{4,3},{5,4},{6,5},{7,6},{8,7},{9,8},{10,9},{11,1... | collective-permute-start | bytes 2359304 | tf_op jit(solution)/shard_map/ppermute | solution.py:28
  443.4 4.9 %copy-start.12 = (f32[512,512]{1,0:T(8,128)S(1)}, f32[512,512]{1,0:T(8,128)}, u32[]{:S(2)}) copy-start(f32[512,512]{1,0:T(8,128)} %get-tuple-element.287) | copy-start | bytes 3145732
  443.4 5.9 %copy-start.11 = (f32[512,512]{1,0:T(8,128)S(1)}, f32[512,512]{1,0:T(8,128)}, u32[]{:S(2)}) copy-start(f32[512,512]{1,0:T(8,128)} %get-tuple-element.288) | copy-start | bytes 3145732
Sparse Core Ops, SparseCore 0:
  211.3 165.8 all-reduce.4
  379.9 27.5 all-reduce.6
